TPU v7x, 256 devices: a whole 4x4x8 slice. The times are simulated.
256 devices in a mesh: grid: 64 (over x_lo, y, z), tm: 4 (over x_hi, core).
Axes of the slice: x: 4 (x_hi: 2, x_lo: 2; x = x_hi * 2 + x_lo), y: 4, z: 8, core: 2. Of those that a mesh axis runs over, the one named last changes fastest.
Arguments:
- temps: float32 [2048, 262144], P('tm', 'grid'), may hold values from -6 to 12
- area_weight: float32 [262144], P('grid'), may hold values from 0.3 to 1
- eofs: bfloat16 [262144, 256], P('grid'), may hold values from -0.03125 to 0.03125
Outputs:
- lag_tiles: float32 [32, 256, 256], P('tm', 'grid')
All inputs are finite; a program needn't handle non-finite values.
Results may differ from a plain program's by a relative error of at most 0.0003.
Values sent between devices are 32-bit elements; how exact they have to be, the bound alone decides.
No kernel may reach another device: no remote copies, remote signals or barrier semaphores. Data moves between devices by JAX's collectives and lax.ppermute only.
A program may use at most 64 MiB of HBM per device.

v0:
```python
import jax
import jax.numpy as jnp
from jax import lax
from jax.sharding import PartitionSpec as P

LAGS = 32


def lagged_columns(own_block, total_rows, first_lag, lag_count):
    empty = jnp.zeros((total_rows, own_block.shape[1]), jnp.float32)
    pieces = [
        lax.dynamic_update_slice_in_dim(empty, own_block, first_lag + offset, 0)
        for offset in range(lag_count)
    ]
    return jnp.concatenate(pieces, axis=1)


def tile_product(own_block, extended, first_lag, lag_count):
    shifted = lagged_columns(own_block, extended.shape[0], first_lag, lag_count)
    product = jnp.einsum("sm,sh->mh", shifted, extended, precision=lax.Precision.HIGHEST)
    return product.reshape(lag_count, own_block.shape[1], extended.shape[1])


def shards(temps, area_weight, eofs):
    hours_dev = temps.shape[0]
    hour_count = hours_dev * lax.axis_size("tm")
    column_sums = lax.psum(jnp.sum(temps, axis=0), "tm")
    column_mean = column_sums / hour_count
    anomaly = ((temps - column_mean) * area_weight).astype(jnp.bfloat16)
    partial_sums = jnp.dot(anomaly, eofs, preferred_element_type=jnp.float32)
    components = lax.psum(partial_sums, "grid")
    channels = components.shape[1]
    chan_block = channels // lax.axis_size("grid")
    chan_start = lax.axis_index("grid") * chan_block
    all_rows = lax.all_gather(components, "tm", axis=0, tiled=True)
    own_block = lax.dynamic_slice_in_dim(all_rows, chan_start, chan_block, 1)
    extended = jnp.concatenate([all_rows, jnp.zeros((LAGS - 1, channels), jnp.float32)], axis=0)
    lag_count = LAGS // lax.axis_size("tm")
    first_lag = lax.axis_index("tm") * lag_count
    lag_tiles = tile_product(own_block, extended, first_lag, lag_count)
    return lag_tiles / hour_count


def solution(mesh):
    placed = (P("tm", "grid"), P("grid"), P("grid", None))
    return jax.shard_map(
        shards, mesh=mesh, in_specs=placed, out_specs=P("tm", "grid", None), check_vma=False
    )
```

profile of v0, /device:TPU:1, one launch (start us, length us, event | category | flops | bytes accessed | tf_op | source)
XLA Modules:
  0.0 680.8 jit_solution(3333425734207268882)
XLA Ops:
  6.5 0.0 copy-start
  6.5 0.0 all-reduce.3.cloned.1.call-start
  6.5 3.9 reduce_sum.9
  10.5 13.5 %psum.14 = f32[4096]{0:T(1024)S(1)} all-reduce(f32[4096]{0:T(1024)S(1)} %reduce_sum.9), channel_id=1, replica_groups=mesh['grid'=64,'tm'=4] {'tm'}, use_global_device_ids=true, to_apply=%region_1.0 | all-reduce | flops 4096 | bytes 32768 | tf_op jit(solution)/shard_map/psum | solution.py:27
  24.0 0.0 copy-done
  24.0 5.4 fusion
  29.4 0.0 all-reduce.3.cloned.1.call-update
  29.4 0.0 all-gather.2.cloned.1.call-start
  29.5 561.3 %all-reduce.3.cloned.1.call-done = f32[512,256]{1,0:T(8,128)} async-done(((f32[512,256]{1,0:T(8,128)}), f32[512,256]{1,0:T(8,128)}) %all-reduce.3.cloned.1.call-update) | async-done | bytes 524304 | tf_op jit(solution)/shard_map/psum | solution.py:31
  590.7 0.0 all-gather.2.cloned.1.call-update
  590.8 73.3 %all-gather.2.cloned.1.call-done = f32[2048,256]{1,0:T(8,128)} async-done(((f32[512,256]{1,0:T(8,128)}), f32[2048,256]{1,0:T(8,128)}) %all-gather.2.cloned.1.call-update) | async-done | bytes 2097168 | tf_op jit(solution)/shard_map/all_gather | solution.py:35
  664.0 1.6 constant_dynamic-slice_fusion
  665.6 0.3 copy.4
  666.0 0.5 dynamic_update_slice.25
  666.5 0.5 dynamic_update_slice.26
  667.1 0.5 dynamic_update_slice.27
  667.7 0.5 dynamic_update_slice.28
  668.2 0.5 dynamic_update_slice.29
  668.8 0.5 dynamic_update_slice.30
  669.4 0.5 dynamic_update_slice.31
  669.9 0.5 dynamic_update_slice.24
  670.5 0.2 concatenate.6
  670.6 2.7 fusion.5
  673.3 0.6 div.18
  (11 shorter events, 0.1 us)
Async XLA Ops:
  6.5 17.4 %copy-start = (bf16[4096,256]{1,0:T(8,128)(2,1)S(1)}, bf16[4096,256]{1,0:T(8,128)(2,1)}, u32[]{:S(2)}) copy-start(bf16[4096,256]{1,0:T(8,128)(2,1)} %param.5) | copy-start | bytes 6291460
  6.5 17.4 %copy-start.1 = (f32[4096]{0:T(1024)S(1)}, f32[4096]{0:T(1024)}, u32[]{:S(2)}) copy-start(f32[4096]{0:T(1024)} %param.4) | copy-start | bytes 49156
  6.5 584.2 %all-reduce.3.cloned.1.call-start = ((), (), s32[]{:S(2)}) async-start(), calls=%async_computation | async-start | bytes 1048576 | tf_op jit(solution)/shard_map/psum | solution.py:31
  29.4 634.6 %all-gather.2.cloned.1.call-start = ((), (), s32[]{:S(2)}) async-start(), calls=%async_computation.1 | async-start | bytes 2621440 | tf_op jit(solution)/shard_map/all_gather | solution.py:35
Sparse Core Ops, SparseCore 0:
  29.5 561.1 all-reduce.2
  592.7 71.3 all-gather.1
where the time goes:
time: 681 us
  waiting for transfers between devices  635 us (93%)
  between operations  13.6 us (2%)
  blocking collectives  13.5 us (2%)
  matrix products  8.09 us (1%)
  local copies, waits for them, and re-layouts  7.09 us (1%)
    psum x1, waiting for transfers between devices, shards(): components = lax.psum(partial_sums, 'grid')  561 us
    all_gather x1, waiting for transfers between devices, shards(): all_rows = lax.all_gather(components, 'tm', axis=0, tiled=True)  73.3 us
  transfers between devices with their start and end apart: 2, of which 2 were waited for; matrix products, arithmetic and copies ran while one was open for 0% of the time, Pallas kernels for 0%

commit v1 on v0

--- a/solution.py
+++ b/solution.py
@@ -28,7 +28,12 @@
     column_mean = column_sums / hour_count
     anomaly = ((temps - column_mean) * area_weight).astype(jnp.bfloat16)
     partial_sums = jnp.dot(anomaly, eofs, preferred_element_type=jnp.float32)
-    components = lax.psum(partial_sums, "grid")
+
+    def see_weights(body):
+        known = lax.all_gather(body, "grid").sum(axis=0)
+        return known
+
+    components = see_weights(partial_sums)
     channels = components.shape[1]
     chan_block = channels // lax.axis_size("grid")
     chan_start = lax.axis_index("grid") * chan_block

time: 681 us -> 468 us (0.69)
  waiting for transfers between devices: 635 us -> 409 us
  other arithmetic: 3.94 us -> 16.6 us
    psum x1 -> x0, waiting for transfers between devices: 561 us -> none  [shards(): components = lax.psum(partial_sums, 'grid')]
    all_gather x0 -> x1, waiting for transfers between devices: none -> 375 us  [see_weights(): known = lax.all_gather(body, 'grid').sum(axis=0)]
    all_gather x1, waiting for transfers between devices: 73.3 us -> 33.4 us  [shards(): all_rows = lax.all_gather(components, 'tm', axis=0, tiled=True)]
    reduce_sum x0 -> x1, other arithmetic: none -> 12.7 us  [see_weights(): known = lax.all_gather(body, 'grid').sum(axis=0)]
where the time goes in v1:
time: 468 us
  waiting for transfers between devices  409 us (87%)
  other arithmetic  16.6 us (4%)
  between operations  13.6 us (3%)
  blocking collectives  13.5 us (3%)
  matrix products  8.1 us (2%)
  local copies, waits for them, and re-layouts  7.09 us (2%)
    all_gather x1, waiting for transfers between devices, see_weights(): known = lax.all_gather(body, 'grid').sum(axis=0)  375 us
    all_gather x1, waiting for transfers between devices, shards(): all_rows = lax.all_gather(components, 'tm', axis=0, tiled=True)  33.4 us
    psum x1, blocking collectives, shards(): column_sums = lax.psum(jnp.sum(temps, axis=0), 'tm')  13.5 us
    reduce_sum x1, other arithmetic, see_weights(): known = lax.all_gather(body, 'grid').sum(axis=0)  12.7 us
  transfers between devices with their start and end apart: 2, of which 2 were waited for; matrix products, arithmetic and copies ran while one was open for 0% of the time, Pallas kernels for 0%

profile of v1, /device:TPU:1, one launch (start us, length us, event | category | flops | bytes accessed | tf_op | source)
XLA Modules:
  0.0 467.7 jit_solution(11292719505856004789)
XLA Ops:
  6.5 0.0 copy-start
  6.5 3.9 reduce_sum.18
  10.5 13.5 %psum.7 = f32[4096]{0:T(1024)S(1)} all-reduce(f32[4096]{0:T(1024)S(1)} %reduce_sum.18), channel_id=1, replica_groups=mesh['grid'=64,'tm'=4] {'tm'}, use_global_device_ids=true, to_apply=%region_1.0 | all-reduce | flops 4096 | bytes 32768 | tf_op jit(solution)/shard_map/psum | solution.py:27
  24.0 0.0 copy-done
  24.0 5.4 %fusion = f32[512,256]{1,0:T(8,128)} fusion(bf16[4096,256]{1,0:T(8,128)(2,1)S(1)} %copy-done, f32[512,4096]{1,0:T(8,128)} %param.3, f32[4096]{0:T(1024)S(1)} %copy-done.1, f32[4096]{0:T(1024)S(1)} %broadcast_multiply_fusion), kind=kOutput, calls=%fused_computation.1 | convolution fusion | flops 1080033280 | bytes 11042816 | tf_op jit(solution)/shard_map/dot_general | solution.py:30
  29.4 0.0 all-gather.6.cloned.1.call-update
  29.4 0.0 all-gather.4.cloned.1.call-start
  29.5 375.5 %all-gather.6.cloned.1.call-done = f32[32768,256]{1,0:T(8,128)} async-done(((f32[512,256]{1,0:T(8,128)}), f32[32768,256]{1,0:T(8,128)}) %all-gather.6.cloned.1.call-update) | async-done | bytes 33554448 | tf_op jit(solution)/shard_map/all_gather | solution.py:33
  405.0 12.7 %reduce_sum.19 = f32[512,256]{1,0:T(8,128)} reduce(f32[64,512,256]{2,1,0:T(8,128)} %bitcast.3, f32[]{:T(128)} %constant.12.clone.1), dimensions={0}, to_apply=%region_2.0 | reduce | flops 8257536 | bytes 34078724 | tf_op jit(solution)/shard_map/reduce_sum | solution.py:33
  417.6 0.0 all-gather.4.cloned.1.call-update
  417.7 33.4 %all-gather.4.cloned.1.call-done = f32[2048,256]{1,0:T(8,128)} async-done(((f32[512,256]{1,0:T(8,128)}), f32[2048,256]{1,0:T(8,128)}) %all-gather.4.cloned.1.call-update) | async-done | bytes 2097168 | tf_op jit(solution)/shard_map/all_gather | solution.py:40
  451.0 1.6 constant_dynamic-slice_fusion
  452.6 0.3 copy.4
  452.9 0.5 dynamic_update_slice.25
  453.5 0.5 dynamic_update_slice.26
  454.1 0.5 dynamic_update_slice.27
  454.6 0.5 dynamic_update_slice.28
  455.2 0.5 dynamic_update_slice.29
  455.8 0.5 dynamic_update_slice.30
  456.3 0.5 dynamic_update_slice.31
  456.9 0.5 dynamic_update_slice.24
  457.5 0.2 concatenate.6
  457.6 2.7 fusion.5
  460.3 0.6 div.18
  (12 shorter events, 0.1 us)
Async XLA Ops:
  6.5 17.4 %copy-start = (bf16[4096,256]{1,0:T(8,128)(2,1)S(1)}, bf16[4096,256]{1,0:T(8,128)(2,1)}, u32[]{:S(2)}) copy-start(bf16[4096,256]{1,0:T(8,128)(2,1)} %param.5) | copy-start | bytes 6291460
  6.5 17.4 %copy-start.1 = (f32[4096]{0:T(1024)S(1)}, f32[4096]{0:T(1024)}, u32[]{:S(2)}) copy-start(f32[4096]{0:T(1024)} %param.4) | copy-start | bytes 49156
  6.5 398.4 %all-gather.6.cloned.1.call-start = ((), (), s32[]{:S(2)}) async-start(), calls=%async_computation.1 | async-start | bytes 34078720 | tf_op jit(solution)/shard_map/all_gather | solution.py:33
  29.4 421.6 %all-gather.4.cloned.1.call-start = ((), (), s32[]{:S(2)}) async-start(), calls=%async_computation | async-start | bytes 2621440 | tf_op jit(solution)/shard_map/all_gather | solution.py:40
Sparse Core Ops, SparseCore 0:
  29.6 375.3 all-gather.5
  417.8 33.1 all-gather.3
